TPU v7x, 32 devices: a whole 2x2x4 slice. The times are simulated.
32 devices in a mesh: groups: 2 (over y), feat: 4 (over z), head: 4 (over x, core).
Axes of the slice: x: 2, y: 2, z: 4, core: 2. Of those that a mesh axis runs over, the one named last changes fastest.
Arguments:
- token_ids: int32 [32], P('groups'), parts along dimension 0, may hold values from 0 to 75967
- embedding: bfloat16 [75968, 5120], P('head', 'feat'), may hold values from -16 to 16
- retained: bfloat16 [2, 32, 8, 8256, 128], P(None, 'groups', 'head', 'feat'), parts along dimension 1, may hold values from -0.29882812 to 0.29882812
- query_weight: bfloat16 [2, 5120, 5120], P(None, 'feat', 'head'), may hold values from -0.078125 to 0.078125
- key_weight: bfloat16 [2, 5120, 1024], P(None, 'feat', 'head'), may hold values from -0.078125 to 0.078125
- value_weight: bfloat16 [2, 5120, 1024], P(None, 'feat', 'head'), may hold values from -0.078125 to 0.078125
- gate_weight: bfloat16 [2, 5120, 8], P(None, 'feat', 'head'), may hold values from -0.078125 to 0.078125
- gate_bias: float32 [2, 8], P(None, 'head'), may hold values from -4 to 3
- norm_gain: float32 [2, 5120], P(None, 'feat'), may hold values from 0.1 to 1.9
- read_gain: float32 [2, 128], replicated, may hold values from 0.1 to 1.9
- out_weight: bfloat16 [2, 5120, 5120], P(None, 'head', 'feat'), may hold values from -0.078125 to 0.078125
Outputs:
- hidden_out: bfloat16 [32, 5120], P('groups', 'feat'), parts along dimension 0
There are 2 independent parts, one for each index of `groups`. A program takes and returns all parts, laid end to end along the dimension named above; an argument that names none is the same for every part. Nothing has to cross between parts.
All inputs are finite; a program needn't handle non-finite values.
Results may differ from a plain program's by a relative error of at most 0.01345.
The roundings to bfloat16 on the way count: a program that leaves them out, or rounds other values in their place, can miss the bound.
Values may be sent and summed in bfloat16 or wider, within the bound.
A program may use at most 192 MiB of HBM per device.

v0:
```python
import functools
import math

import jax
import jax.numpy as jnp
from jax import lax
from jax.experimental import pallas as pl
from jax.experimental.pallas import tpu as pltpu
from jax.sharding import PartitionSpec as P

MESH = pl.DeviceIdType.MESH
F32 = jnp.float32
BF16 = jnp.bfloat16
SEND = jnp.bfloat16


def lookup(ids_ref, table_hbm, picked_ref, rows_buf, row_sem):
    requests, width = picked_ref.shape
    table_rows = table_hbm.shape[0]
    base = lax.axis_index("head") * table_rows
    window = rows_buf.shape[0] // requests
    out_row = lax.broadcasted_iota(jnp.int32, (requests, requests * window), 0)
    column = lax.broadcasted_iota(jnp.int32, (requests, requests * window), 1)
    select = jnp.zeros((requests, requests * window), F32)
    copies = []
    for i in range(requests):
        local = ids_ref[i] - base
        row = jnp.clip(local, 0, table_rows - 1)
        first = pl.multiple_of(jnp.minimum((row // 8) * 8, table_rows - window), 8)
        copy = pltpu.make_async_copy(
            table_hbm.at[pl.ds(first, window)],
            rows_buf.at[pl.ds(i * window, window)],
            row_sem.at[i],
        )
        copy.start()
        copies.append(copy)
        value = jnp.where(local == row, 1.0, 0.0)
        hit = (out_row == i) & (column == i * window + row - first)
        select = jnp.where(hit, value, select)
    for copy in copies:
        copy.wait()
    picked_ref[...] = jnp.dot(
        select.astype(BF16), rows_buf[...], preferred_element_type=F32
    ).astype(BF16)


def partner_of(me, count, turn):
    if count == 4:
        return (3 - me, lax.rem(me + 2, 4), me + 1 - 2 * lax.rem(me, 2))[turn - 1]
    return lax.rem(me + turn, count)


def kernel(
    feat_count,
    head_count,
    picked_ref,
    retained_hbm,
    query_hbm,
    key_hbm,
    value_hbm,
    gate_hbm,
    bias_ref,
    gain_ref,
    read_ref,
    out_hbm,
    result_ref,
    state,
    query_w,
    key_w,
    value_w,
    gate_w,
    out_w,
    pick_buf,
    query_buf,
    pair_buf,
    small_buf,
    read_buf,
    branch_buf,
    left_sel,
    right_sel,
    pair_scale,
    phi,
    history,
    partial,
    load_sem,
    state_sem,
    send_sem,
    recv_sem,
):
    layers, requests, heads, block, head_size = state.shape
    width = query_w.shape[1]
    query_columns = query_w.shape[2]
    kv_columns = key_w.shape[2]
    chunks, chunk = branch_buf.shape[1], branch_buf.shape[4]
    group = query_columns // (heads * head_size)
    me_feat = lax.axis_index("feat")
    me_head = lax.axis_index("head")

    load = {}

    def load_inputs(layer):
        pairs = [(gate_hbm, gate_w), (query_hbm, query_w), (key_hbm, key_w), (value_hbm, value_w)]
        for slot, (source, target) in enumerate(pairs):
            load[layer, slot] = pltpu.make_async_copy(
                source.at[layer], target.at[layer], load_sem.at[layer, slot]
            )
            load[layer, slot].start()

    def load_state(layer):
        for r in range(requests):
            pltpu.make_async_copy(
                retained_hbm.at[layer, r], state.at[layer, r], state_sem.at[layer, r]
            ).start()
        load[layer, 4] = pltpu.make_async_copy(
            out_hbm.at[layer], out_w.at[layer], load_sem.at[layer, 4]
        )
        load[layer, 4].start()

    load_inputs(0)

    barrier = pltpu.get_barrier_semaphore()
    for axis, count, me in (("feat", feat_count, me_feat), ("head", head_count, me_head)):
        for d in range(1, count):
            pl.semaphore_signal(
                barrier, inc=1, device_id={axis: lax.rem(me + d, count)}, device_id_type=MESH
            )
    pl.semaphore_wait(barrier, feat_count + head_count - 2)

    used = [0]

    def exchange(axis, count, me, source_of, target):
        copies = []
        for d in range(1, count):
            copy = pltpu.make_async_remote_copy(
                src_ref=source_of,
                dst_ref=target,
                send_sem=send_sem.at[used[0]],
                recv_sem=recv_sem.at[used[0]],
                device_id={axis: partner_of(me, count, d)},
                device_id_type=MESH,
            )
            copy.start()
            copies.append(copy)
            used[0] += 1
        return copies

    pending = exchange("head", head_count, me_head, picked_ref, pick_buf.at[me_head])
    load_state(0)
    pick_buf[me_head] = picked_ref[...]

    feature = lax.broadcasted_iota(jnp.int32, (head_size, block), 1) + me_feat * block
    position = lax.broadcasted_iota(jnp.int32, (head_size, block), 0)
    begin = position * head_size - (position * (position - 1)) // 2
    inside = (feature >= begin) & (feature < begin + head_size - position)
    left_sel[...] = jnp.where(inside, 1.0, 0.0).astype(BF16)
    partner = jnp.sum(jnp.where(inside, feature - begin + position, 0), axis=0, keepdims=True)
    right_sel[...] = jnp.where(position == partner, 1.0, 0.0).astype(BF16)
    first = jnp.sum(jnp.where(inside, position, 0), axis=0, keepdims=True)
    pair_scale[...] = jnp.where(first == partner, 1.0, math.sqrt(2.0)).astype(F32)

    slots = requests * 8
    compact = requests * group
    span = group * head_size
    unroll = 4 if requests % 4 == 0 else 1

    def place(rows, columns, swap):
        a = lax.broadcasted_iota(jnp.int32, (rows, columns), 0)
        b = lax.broadcasted_iota(jnp.int32, (rows, columns), 1)
        wide, packed = (b, a) if swap else (a, b)
        match = (packed == (wide % 8) * requests + wide // 8) & (wide % 8 < group)
        return jnp.where(match, 1.0, 0.0).astype(BF16)

    spread = place(slots, compact, False)
    gather = place(compact, slots, True)

    for copy in pending:
        copy.wait()
    stream = pick_buf[0].astype(F32)
    for i in range(1, head_count):
        stream = stream + pick_buf[i].astype(F32)

    for layer in range(layers):
        gained = (stream * gain_ref[layer : layer + 1, :]).astype(BF16)
        square = jnp.sum(stream * stream, axis=1, keepdims=True)
        load[layer, 0].wait()
        gained_wide = gained.astype(F32)
        gates = gate_w[layer].astype(F32)
        lane = lax.broadcasted_iota(jnp.int32, (requests, 128), 1)
        small = jnp.where(lane == heads, square, 0.0)
        for h in range(heads):
            along = jnp.sum(gained_wide * gates[h : h + 1, :], axis=1, keepdims=True)
            small = jnp.where(lane == h, along, small)
        small_buf[layer, me_feat] = small
        small_copies = exchange(
            "feat", feat_count, me_feat, small_buf.at[layer, me_feat], small_buf.at[layer, me_feat]
        )
        load[layer, 1].wait()
        query_copies = []
        for h in range(heads):
            query_buf[layer, h, me_feat] = jnp.dot(
                gained, query_w[layer, :, h * span : (h + 1) * span], preferred_element_type=F32
            ).astype(SEND)
            own = query_buf.at[layer, h, me_feat]
            query_copies.append(exchange("feat", feat_count, me_feat, own, own))
        for slot, weight in ((2, key_w), (3, value_w)):
            load[layer, slot].wait()
            pair_buf[layer, me_feat, :, (slot - 2) * kv_columns : (slot - 1) * kv_columns] = jnp.dot(
                gained, weight[layer], preferred_element_type=F32
            ).astype(SEND)
        own = pair_buf.at[layer, me_feat]
        pair_copies = exchange("feat", feat_count, me_feat, own, own)
        if layer + 1 < layers:
            load_inputs(layer + 1)
            load_state(layer + 1)
        for copy in small_copies:
            copy.wait()
        totals = small_buf[layer, 0]
        for i in range(1, feat_count):
            totals = totals + small_buf[layer, i]
        inverse = lax.rsqrt(totals[:, heads : heads + 1] / (width * feat_count) + 1e-06)
        gate = totals[:, :heads] * inverse + bias_ref[layer : layer + 1, :]
        decay = 1.0 / (1.0 + jnp.exp(gate))
        query = []
        read_copies = []
        for h in range(heads):
            for copy in query_copies[h]:
                copy.wait()
            summed = query_buf[layer, h, 0].astype(F32)
            for i in range(1, feat_count):
                summed = summed + query_buf[layer, h, i].astype(F32)
            summed = (summed * inverse).astype(BF16)
            rows = [summed[:, i * head_size : (i + 1) * head_size] for i in range(group)]
            query.append(rows)
            stacked = jnp.concatenate(rows, axis=0)
            placed = jnp.dot(spread, stacked, preferred_element_type=F32).astype(BF16)
            for start in range(0, block, 256):
                stop = min(start + 256, block)
                left = jnp.dot(placed, left_sel[:, start:stop], preferred_element_type=F32)
                right = jnp.dot(placed, right_sel[:, start:stop], preferred_element_type=F32)
                phi[:, start:stop] = left * right * pair_scale[:, start:stop]

            def read(step, carry, h=h):
                for extra in range(unroll):
                    r = step * unroll + extra
                    if h == 0:
                        pltpu.make_async_copy(
                            retained_hbm.at[layer, r], state.at[layer, r], state_sem.at[layer, r]
                        ).wait()
                for extra in range(unroll):
                    r = step * unroll + extra
                    at = pl.ds(pl.multiple_of(r * 8, 8), 8)
                    history[at, :] = jnp.dot(
                        phi[at, :].astype(BF16), state[layer, r, h], preferred_element_type=F32
                    )
                return carry

            lax.fori_loop(0, requests // unroll, read, 0)
            packed = jnp.dot(gather, history[...].astype(BF16), preferred_element_type=F32)
            read_buf[layer, h, me_feat] = packed.astype(SEND)
            own = read_buf.at[layer, h, me_feat]
            read_copies.append(exchange("feat", feat_count, me_feat, own, own))
        for copy in pair_copies:
            copy.wait()
        summed = pair_buf[layer, 0].astype(F32)
        for i in range(1, feat_count):
            summed = summed + pair_buf[layer, i].astype(F32)
        summed = (summed * inverse).astype(BF16).astype(F32)
        branch_copies = []
        load[layer, 4].wait()
        for h in range(heads):
            key = summed[:, h * head_size : (h + 1) * head_size]
            value = summed[:, kv_columns + h * head_size : kv_columns + (h + 1) * head_size]
            cross = []
            for i in range(group):
                along = jnp.sum(query[h][i].astype(F32) * key, axis=1, keepdims=True)
                cross.append(along * along / head_size)
            for copy in read_copies[h]:
                copy.wait()
            reads = read_buf[layer, h, 0].astype(F32)
            for i in range(1, feat_count):
                reads = reads + read_buf[layer, h, i].astype(F32)
            mixed = []
            for i in range(group):
                readout = (
                    decay[:, h : h + 1] * reads[i * requests : (i + 1) * requests]
                    + cross[i] * value
                )
                scale = lax.rsqrt(jnp.mean(readout * readout, axis=1, keepdims=True) + 1e-06)
                mixed.append((readout * scale * read_ref[layer : layer + 1, :]).astype(BF16))
            mixed = jnp.concatenate(mixed, axis=1)
            for c in range(chunks):
                columns = slice(c * chunk, (c + 1) * chunk)
                part = jnp.dot(
                    mixed,
                    out_w[layer, h * span : (h + 1) * span, columns],
                    preferred_element_type=F32,
                )
                if h > 0:
                    part = part + partial[:, columns]
                if h < heads - 1:
                    partial[:, columns] = part
                else:
                    branch_buf[layer, c, me_head] = part.astype(SEND)
                    own = branch_buf.at[layer, c, me_head]
                    branch_copies.append(exchange("head", head_count, me_head, own, own))
        branch = []
        for c in range(chunks):
            for copy in branch_copies[c]:
                copy.wait()
            total = branch_buf[layer, c, 0].astype(F32)
            for i in range(1, head_count):
                total = total + branch_buf[layer, c, i].astype(F32)
            branch.append(total)
        branch = jnp.concatenate(branch, axis=1) if chunks > 1 else branch[0]
        stream_out = (stream + branch).astype(BF16)
        stream = stream_out.astype(F32)
    result_ref[...] = stream_out


def body(
    feat_count,
    head_count,
    token_ids,
    embedding,
    retained,
    query_weight,
    key_weight,
    value_weight,
    gate_weight,
    gate_bias,
    norm_gain,
    read_gain,
    out_weight,
):
    layers, requests, heads, block, head_size = retained.shape
    width = query_weight.shape[1]
    query_columns = query_weight.shape[2]
    kv_columns = key_weight.shape[2]
    group = query_columns // (heads * head_size)
    chunks = 2 if width % 256 == 0 else 1
    copies = (head_count - 1) + layers * (
        (2 + 2 * heads) * (feat_count - 1) + chunks * (head_count - 1)
    )
    gate_rows = jnp.swapaxes(gate_weight, 1, 2)
    window = 16
    picked = pl.pallas_call(
        lookup,
        out_shape=jax.ShapeDtypeStruct((requests, width), BF16),
        in_specs=[pl.BlockSpec(memory_space=pltpu.SMEM), pl.BlockSpec(memory_space=pl.ANY)],
        out_specs=pl.BlockSpec(memory_space=pltpu.VMEM),
        scratch_shapes=[
            pltpu.VMEM((requests * window, width), BF16),
            pltpu.SemaphoreType.DMA((requests,)),
        ],
    )(token_ids, embedding)
    anywhere = pl.BlockSpec(memory_space=pl.ANY)
    local = pl.BlockSpec(memory_space=pltpu.VMEM)
    return pl.pallas_call(
        functools.partial(kernel, feat_count, head_count),
        out_shape=jax.ShapeDtypeStruct((requests, width), BF16),
        in_specs=[local] + [anywhere] * 5 + [local] * 3 + [anywhere],
        out_specs=local,
        scratch_shapes=[
            pltpu.VMEM(retained.shape, BF16),
            pltpu.VMEM(query_weight.shape, BF16),
            pltpu.VMEM(key_weight.shape, BF16),
            pltpu.VMEM(value_weight.shape, BF16),
            pltpu.VMEM(gate_rows.shape, BF16),
            pltpu.VMEM(out_weight.shape, BF16),
            pltpu.VMEM((head_count, requests, width), BF16),
            pltpu.VMEM((layers, heads, feat_count, requests, group * head_size), SEND),
            pltpu.VMEM((layers, feat_count, requests, 2 * kv_columns), SEND),
            pltpu.VMEM((layers, feat_count, requests, 128), F32),
            pltpu.VMEM((layers, heads, feat_count, requests * group, head_size), SEND),
            pltpu.VMEM((layers, chunks, head_count, requests, width // chunks), SEND),
            pltpu.VMEM((head_size, block), BF16),
            pltpu.VMEM((head_size, block), BF16),
            pltpu.VMEM((1, block), F32),
            pltpu.VMEM((requests * 8, block), F32),
            pltpu.VMEM((requests * 8, head_size), F32),
            pltpu.VMEM((requests, width), F32),
            pltpu.SemaphoreType.DMA((layers, 5)),
            pltpu.SemaphoreType.DMA((layers, requests)),
            pltpu.SemaphoreType.DMA((copies,)),
            pltpu.SemaphoreType.DMA((copies,)),
        ],
        compiler_params=pltpu.CompilerParams(
            collective_id=0, has_side_effects=True, vmem_limit_bytes=66_000_000
        ),
    )(
        picked,
        retained,
        query_weight,
        key_weight,
        value_weight,
        gate_rows,
        gate_bias,
        norm_gain,
        read_gain,
        out_weight,
    )


def solution(mesh):
    return jax.shard_map(
        functools.partial(body, mesh.shape["feat"], mesh.shape["head"]),
        mesh=mesh,
        in_specs=(
            P("groups"),
            P("head", "feat"),
            P(None, "groups", "head", "feat", None),
            P(None, "feat", "head"),
            P(None, "feat", "head"),
            P(None, "feat", "head"),
            P(None, "feat", "head"),
            P(None, "head"),
            P(None, "feat"),
            P(),
            P(None, "head", "feat"),
        ),
        out_specs=P("groups", "feat"),
        check_vma=False,
    )
```

profile of v0, /device:TPU:0, one launch (start us, length us, event | category | flops | bytes accessed | tf_op | source)
XLA Modules:
  0.0 53.8 jit_solution(13778521845664550036)
XLA Ops:
  0.0 3.3 %shard_map.109.picked_ref = bf16[16,1280]{1,0:T(8,128)(2,1)} custom-call(s32[16]{0:T(128)} %ids_ref.1, bf16[18992,1280]{1,0:T(8,128)(2,1)} %table_hbm.1), custom_call_target="tpu_custom_call" | custom-call | tf_op jit(solution)/shard_map/pallas_call | solution.py:346
  3.3 49.1 %shard_map.110 = bf16[16,1280]{1,0:T(8,128)(2,1)} custom-call(bf16[16,1280]{1,0:T(8,128)(2,1)} %shard_map.109.picked_ref, bf16[2,16,2,2064,128]{4,3,2,1,0:T(8,128)(2,1)} %retained_hbm.1, bf16[2,1280,1280]{2,1,0:T(8,128)(2,1)} %query_hbm.1, bf16[2,1280,256]{2,1,0:T(8,128)(2,1)} %key_hbm.1, bf16[2,1280,256]{2,1,0:T(8,128)(2,1)} %value_hbm.1, ...), custom_call_target="tpu_custom_call" | custom-call | tf_op jit(solution)/shard_map/pallas_call | solution.py:358
  52.4 1.4 %copy.13 = bf16[16,1280]{1,0:T(8,128)(2,1)} copy(bf16[16,1280]{1,0:T(8,128)(2,1)} %shard_map.110) | data formatting | bytes 81920
where the time goes:
time: 54.2 us; the launch traced here: 53.8 us
  Pallas kernels  52.4 us (97%)
  local copies, waits for them, and re-layouts  1.4 us (3%)
    pallas_call x1, Pallas kernels, body(): pl.pallas_call(functools.partial(kernel, feat_count, head_count), out_sha...  49.1 us
    pallas_call x1, Pallas kernels, body(): pl.pallas_call(lookup, out_shape=jax.ShapeDtypeStruct((requests, width),...  3.25 us
    unnamed x1, local copies, waits for them, and re-layouts  1.4 us

commit v1 on v0

v1 whole, which is shorter than its diff:
```python
import functools
import math

import jax
import jax.numpy as jnp
from jax import lax
from jax.experimental import pallas as pl
from jax.experimental.pallas import tpu as pltpu
from jax.sharding import PartitionSpec as P

MESH = pl.DeviceIdType.MESH
F32 = jnp.float32
BF16 = jnp.bfloat16
LANES = 128


def lookup(ids_ref, table_hbm, picked_ref, rows_buf, row_sem):
    requests, width = picked_ref.shape
    table_rows = table_hbm.shape[0]
    base = lax.axis_index("head") * table_rows
    window = rows_buf.shape[0] // requests
    out_row = lax.broadcasted_iota(jnp.int32, (requests, requests * window), 0)
    column = lax.broadcasted_iota(jnp.int32, (requests, requests * window), 1)
    select = jnp.zeros((requests, requests * window), F32)
    copies = []
    for i in range(requests):
        local = ids_ref[i] - base
        row = jnp.clip(local, 0, table_rows - 1)
        first = pl.multiple_of(jnp.minimum((row // 8) * 8, table_rows - window), 8)
        copy = pltpu.make_async_copy(
            table_hbm.at[pl.ds(first, window)],
            rows_buf.at[pl.ds(i * window, window)],
            row_sem.at[i],
        )
        copy.start()
        copies.append(copy)
        value = jnp.where(local == row, 1.0, 0.0)
        hit = (out_row == i) & (column == i * window + row - first)
        select = jnp.where(hit, value, select)
    for copy in copies:
        copy.wait()
    picked_ref[...] = jnp.dot(
        select.astype(BF16), rows_buf[...], preferred_element_type=F32
    ).astype(BF16)


def partner_of(me, count, turn):
    if count == 4:
        return (3 - me, lax.rem(me + 2, 4), me + 1 - 2 * lax.rem(me, 2))[turn - 1]
    return lax.rem(me + turn, count)


def kernel(
    feat_count,
    head_count,
    parts,
    picked_ref,
    retained_hbm,
    query_hbm,
    key_hbm,
    value_hbm,
    gate_hbm,
    bias_hbm,
    gain_hbm,
    read_hbm,
    out_hbm,
    result_ref,
    state,
    query_w,
    key_w,
    value_w,
    gate_w,
    bias_ref,
    gain_ref,
    read_ref,
    out_w,
    pick_buf,
    lead_buf,
    query_buf,
    pair_buf,
    read_buf,
    branch_buf,
    left_sel,
    right_sel,
    pair_scale,
    phi,
    history,
    load_sem,
    state_sem,
    send_sem,
    recv_sem,
):
    layers, requests, heads, block, head_size = state.shape
    width = query_w.shape[1]
    query_columns = query_w.shape[2]
    kv_columns = key_w.shape[2]
    chunks, chunk = branch_buf.shape[2], branch_buf.shape[5]
    group = query_columns // (heads * head_size)
    span = group * head_size
    n = requests // parts
    me_feat = lax.axis_index("feat")
    me_head = lax.axis_index("head")

    barrier = pltpu.get_barrier_semaphore()
    for axis, count, me in (("feat", feat_count, me_feat), ("head", head_count, me_head)):
        for d in range(1, count):
            pl.semaphore_signal(
                barrier, inc=1, device_id={axis: lax.rem(me + d, count)}, device_id_type=MESH
            )

    load = {}

    def start_load(slot, source, target, layer):
        load[layer, slot] = pltpu.make_async_copy(source, target, load_sem.at[layer, slot])
        load[layer, slot].start()

    def load_inputs(layer):
        pairs = [(gate_hbm, gate_w), (query_hbm, query_w), (key_hbm, key_w), (value_hbm, value_w)]
        for slot, (source, target) in enumerate(pairs):
            start_load(slot, source.at[layer], target.at[layer], layer)

    def load_state(layer):
        for r in range(requests):
            pltpu.make_async_copy(
                retained_hbm.at[layer, r], state.at[layer, r], state_sem.at[layer, r]
            ).start()
        start_load(4, out_hbm.at[layer], out_w.at[layer], layer)

    start_load(5, gain_hbm, gain_ref, 0)
    start_load(6, bias_hbm, bias_ref, 0)
    start_load(7, read_hbm, read_ref, 0)
    load_inputs(0)
    pl.semaphore_wait(barrier, feat_count + head_count - 2)

    sent = []

    def exchange(axis, count, me, source, target):
        copies = []
        for d in range(1, count):
            copy = pltpu.make_async_remote_copy(
                src_ref=source,
                dst_ref=target,
                send_sem=send_sem.at[len(sent)],
                recv_sem=recv_sem.at[len(sent)],
                device_id={axis: partner_of(me, count, d)},
                device_id_type=MESH,
            )
            copy.start()
            copies.append(copy)
            sent.append(copy)
        return copies

    def arrive(copies):
        for copy in copies:
            copy.wait_recv()

    pick_copies = []
    for p in range(parts):
        rows = slice(p * n, (p + 1) * n)
        pick_copies.append(
            exchange(
                "head", head_count, me_head, picked_ref.at[rows], pick_buf.at[p, me_head]
            )
        )
    load_state(0)
    for layer in range(1, layers):
        load_inputs(layer)
        load_state(layer)

    feature = lax.broadcasted_iota(jnp.int32, (head_size, block), 1) + me_feat * block
    position = lax.broadcasted_iota(jnp.int32, (head_size, block), 0)
    begin = position * head_size - (position * (position - 1)) // 2
    inside = (feature >= begin) & (feature < begin + head_size - position)
    left_sel[...] = jnp.where(inside, 1.0, 0.0).astype(BF16)
    partner = jnp.sum(jnp.where(inside, feature - begin + position, 0), axis=0, keepdims=True)
    right_sel[...] = jnp.where(position == partner, 1.0, 0.0).astype(BF16)
    first = jnp.sum(jnp.where(inside, position, 0), axis=0, keepdims=True)
    pair_scale[...] = jnp.where(first == partner, 1.0, math.sqrt(2.0)).astype(F32)
    phi[...] = jnp.zeros(phi.shape, F32)

    for slot in (5, 6, 7):
        load[0, slot].wait()

    fields = heads + 1
    lane = lax.broadcasted_iota(jnp.int32, (n, LANES), 1)
    unroll = 4 if n % 4 == 0 else 1
    stream = [None] * parts
    branch_copies = [None] * parts

    for p in range(parts):
        pick_buf[p, me_head] = picked_ref[p * n : (p + 1) * n, :]

    for layer in range(layers):
        lead_copies, query_copies, pair_copies = [], [], []
        for p in range(parts):
            if layer == 0:
                arrive(pick_copies[p])
                total = pick_buf[p, 0].astype(F32)
                for i in range(1, head_count):
                    total = total + pick_buf[p, i].astype(F32)
                stream[p] = total
            else:
                stream[p] = finish(p, layer - 1, stream, branch_copies, branch_buf, head_count, arrive)
            gained = (stream[p] * gain_ref[layer : layer + 1, :]).astype(BF16)
            if p == 0:
                load[layer, 0].wait()
                load[layer, 1].wait()
            lead_buf[layer, p, me_feat, :, :span] = jnp.dot(
                gained, query_w[layer, :, :span], preferred_element_type=F32
            ).astype(BF16)
            values = [jnp.sum(stream[p] * stream[p], axis=1, keepdims=True)]
            gained_wide = gained.astype(F32)
            gates = gate_w[layer].astype(F32)
            for h in range(heads):
                values.append(jnp.sum(gained_wide * gates[h : h + 1, :], axis=1, keepdims=True))
            small = jnp.zeros((n, LANES), F32)
            for k, value in enumerate(values):
                spots = (lane == k) | (lane == fields + k) | (lane == 2 * fields + k)
                small = jnp.where(spots, value, small)
            high = small.astype(BF16).astype(F32)
            rest = small - high
            middle = rest.astype(BF16).astype(F32)
            lead_buf[layer, p, me_feat, :, span:] = jnp.where(
                lane < fields, high, jnp.where(lane < 2 * fields, middle, rest - middle)
            ).astype(BF16)
            own = lead_buf.at[layer, p, me_feat]
            lead_copies.append(exchange("feat", feat_count, me_feat, own, own))
            copies = []
            for h in range(1, heads):
                query_buf[layer, p, h - 1, me_feat] = jnp.dot(
                    gained, query_w[layer, :, h * span : (h + 1) * span], preferred_element_type=F32
                ).astype(BF16)
                own = query_buf.at[layer, p, h - 1, me_feat]
                copies.append(exchange("feat", feat_count, me_feat, own, own))
            query_copies.append(copies)
            for slot, weight in ((2, key_w), (3, value_w)):
                if p == 0:
                    load[layer, slot].wait()
                pair_buf[layer, p, me_feat, :, (slot - 2) * kv_columns : (slot - 1) * kv_columns] = (
                    jnp.dot(gained, weight[layer], preferred_element_type=F32).astype(BF16)
                )
            own = pair_buf.at[layer, p, me_feat]
            pair_copies.append(exchange("feat", feat_count, me_feat, own, own))

        query, decay, inverse, read_copies = [], [], [], []
        for p in range(parts):
            arrive(lead_copies[p])
            totals = lead_buf[layer, p, 0, :, span:].astype(F32)
            for i in range(1, feat_count):
                totals = totals + lead_buf[layer, p, i, :, span:].astype(F32)
            totals = (
                totals
                + pltpu.roll(totals, LANES - fields, 1)
                + pltpu.roll(totals, LANES - 2 * fields, 1)
            )
            inverse.append(lax.rsqrt(totals[:, :1] / (width * feat_count) + 1e-06))
            gate = totals[:, 1 : 1 + heads] * inverse[p] + bias_ref[layer : layer + 1, :]
            decay.append(1.0 / (1.0 + jnp.exp(gate)))
            query.append([])
            read_copies.append([])
            for h in range(heads):
                if h == 0:
                    summed = lead_buf[layer, p, 0, :, :span].astype(F32)
                    for i in range(1, feat_count):
                        summed = summed + lead_buf[layer, p, i, :, :span].astype(F32)
                else:
                    arrive(query_copies[p][h - 1])
                    summed = query_buf[layer, p, h - 1, 0].astype(F32)
                    for i in range(1, feat_count):
                        summed = summed + query_buf[layer, p, h - 1, i].astype(F32)
                summed = summed * inverse[p]
                rows = [summed[:, i * head_size : (i + 1) * head_size] for i in range(group)]
                stacked = jnp.concatenate(rows, axis=0).astype(BF16)
                query[p].append([row.astype(BF16).astype(F32) for row in rows])
                for start in range(0, block, 256):
                    stop = min(start + 256, block)
                    left = jnp.dot(stacked, left_sel[:, start:stop], preferred_element_type=F32)
                    right = jnp.dot(stacked, right_sel[:, start:stop], preferred_element_type=F32)
                    value = left * right * pair_scale[:, start:stop]
                    for lo in range(start, stop, LANES):
                        hi = min(lo + LANES, stop)
                        phi[lo // LANES, : group * n, : hi - lo] = value[:, lo - start : hi - start]

                def read(step, carry, h=h, p=p):
                    if h == 0:
                        for extra in range(unroll):
                            r = p * n + step * unroll + extra
                            pltpu.make_async_copy(
                                retained_hbm.at[layer, r], state.at[layer, r], state_sem.at[layer, r]
                            ).wait()
                    for extra in range(unroll):
                        i = step * unroll + extra
                        at = pl.ds(i, 8, stride=n)
                        lhs = jnp.concatenate(
                            [phi[c, at, :] for c in range(phi.shape[0])], axis=1
                        )[:, :block]
                        history[at, :] = jnp.dot(
                            lhs.astype(BF16), state[layer, p * n + i, h], preferred_element_type=F32
                        )
                    return carry

                lax.fori_loop(0, n // unroll, read, 0)
                read_buf[layer, p, h, me_feat] = history[: group * n, :].astype(BF16)
                own = read_buf.at[layer, p, h, me_feat]
                read_copies[p].append(exchange("feat", feat_count, me_feat, own, own))

        for p in range(parts):
            arrive(pair_copies[p])
            summed = pair_buf[layer, p, 0].astype(F32)
            for i in range(1, feat_count):
                summed = summed + pair_buf[layer, p, i].astype(F32)
            summed = (summed * inverse[p]).astype(BF16).astype(F32)
            if p == 0:
                load[layer, 4].wait()
            branch_copies[p] = []
            partial = None
            for h in range(heads):
                key = summed[:, h * head_size : (h + 1) * head_size]
                value = summed[:, kv_columns + h * head_size : kv_columns + (h + 1) * head_size]
                cross = []
                for i in range(group):
                    along = jnp.sum(query[p][h][i] * key, axis=1, keepdims=True)
                    cross.append(along * along / head_size)
                arrive(read_copies[p][h])
                reads = read_buf[layer, p, h, 0].astype(F32)
                for i in range(1, feat_count):
                    reads = reads + read_buf[layer, p, h, i].astype(F32)
                mixed = []
                for i in range(group):
                    readout = (
                        decay[p][:, h : h + 1] * reads[i * n : (i + 1) * n] + cross[i] * value
                    )
                    scale = lax.rsqrt(jnp.mean(readout * readout, axis=1, keepdims=True) + 1e-06)
                    mixed.append((readout * scale * read_ref[layer : layer + 1, :]).astype(BF16))
                mixed = jnp.concatenate(mixed, axis=1)
                pieces = []
                for c in range(chunks):
                    part = jnp.dot(
                        mixed,
                        out_w[layer, h * span : (h + 1) * span, c * chunk : (c + 1) * chunk],
                        preferred_element_type=F32,
                    )
                    if h > 0:
                        part = part + partial[c]
                    pieces.append(part)
                    if h == heads - 1:
                        branch_buf[layer, p, c, me_head] = part.astype(BF16)
                        own = branch_buf.at[layer, p, c, me_head]
                        branch_copies[p].append(exchange("head", head_count, me_head, own, own))
                partial = pieces

    for p in range(parts):
        done = finish(p, layers - 1, stream, branch_copies, branch_buf, head_count, arrive)
        result_ref[p * n : (p + 1) * n, :] = done.astype(BF16)
    for copy in sent:
        copy.wait_send()


def finish(p, layer, stream, branch_copies, branch_buf, head_count, arrive):
    branch = []
    for c in range(len(branch_copies[p])):
        arrive(branch_copies[p][c])
        total = branch_buf[layer, p, c, 0].astype(F32)
        for i in range(1, head_count):
            total = total + branch_buf[layer, p, c, i].astype(F32)
        branch.append(total)
    branch = jnp.concatenate(branch, axis=1) if len(branch) > 1 else branch[0]
    return (stream[p] + branch).astype(BF16).astype(F32)


def body(
    feat_count,
    head_count,
    token_ids,
    embedding,
    retained,
    query_weight,
    key_weight,
    value_weight,
    gate_weight,
    gate_bias,
    norm_gain,
    read_gain,
    out_weight,
):
    layers, requests, heads, block, head_size = retained.shape
    width = query_weight.shape[1]
    query_columns = query_weight.shape[2]
    kv_columns = key_weight.shape[2]
    group = query_columns // (heads * head_size)
    span = group * head_size
    parts = 2 if requests % 16 == 0 else 1
    n = requests // parts
    chunks = 1
    copies = parts * (
        (head_count - 1)
        + layers * ((1 + 2 * heads) * (feat_count - 1) + chunks * (head_count - 1))
    )
    gate_rows = jnp.swapaxes(gate_weight, 1, 2)
    window = 16
    picked = pl.pallas_call(
        lookup,
        out_shape=pltpu.VMEM((requests, width), BF16),
        in_specs=[pl.BlockSpec(memory_space=pltpu.SMEM), pl.BlockSpec(memory_space=pl.ANY)],
        out_specs=pl.BlockSpec(memory_space=pltpu.VMEM),
        scratch_shapes=[
            pltpu.VMEM((requests * window, width), BF16),
            pltpu.SemaphoreType.DMA((requests,)),
        ],
    )(token_ids, embedding)
    anywhere = pl.BlockSpec(memory_space=pl.ANY)
    local = pl.BlockSpec(memory_space=pltpu.VMEM)
    return pl.pallas_call(
        functools.partial(kernel, feat_count, head_count, parts),
        out_shape=pltpu.VMEM((requests, width), BF16),
        in_specs=[local] + [anywhere] * 9,
        out_specs=local,
        scratch_shapes=[
            pltpu.VMEM(retained.shape, BF16),
            pltpu.VMEM(query_weight.shape, BF16),
            pltpu.VMEM(key_weight.shape, BF16),
            pltpu.VMEM(value_weight.shape, BF16),
            pltpu.VMEM(gate_rows.shape, BF16),
            pltpu.VMEM(gate_bias.shape, F32),
            pltpu.VMEM(norm_gain.shape, F32),
            pltpu.VMEM(read_gain.shape, F32),
            pltpu.VMEM(out_weight.shape, BF16),
            pltpu.VMEM((parts, head_count, n, width), BF16),
            pltpu.VMEM((layers, parts, feat_count, n, span + LANES), BF16),
            pltpu.VMEM((layers, parts, max(heads - 1, 1), feat_count, n, span), BF16),
            pltpu.VMEM((layers, parts, feat_count, n, 2 * kv_columns), BF16),
            pltpu.VMEM((layers, parts, heads, feat_count, n * group, head_size), BF16),
            pltpu.VMEM((layers, parts, chunks, head_count, n, width // chunks), BF16),
            pltpu.VMEM((head_size, block), BF16),
            pltpu.VMEM((head_size, block), BF16),
            pltpu.VMEM((1, block), F32),
            pltpu.VMEM((pl.cdiv(block, LANES), 8 * n, LANES), F32),
            pltpu.VMEM((8 * n, head_size), F32),
            pltpu.SemaphoreType.DMA((layers, 8)),
            pltpu.SemaphoreType.DMA((layers, requests)),
            pltpu.SemaphoreType.DMA((copies,)),
            pltpu.SemaphoreType.DMA((copies,)),
        ],
        compiler_params=pltpu.CompilerParams(
            collective_id=0, has_side_effects=True, vmem_limit_bytes=66_000_000
        ),
    )(
        pltpu.with_memory_space_constraint(picked, pltpu.VMEM),
        retained,
        query_weight,
        key_weight,
        value_weight,
        gate_rows,
        gate_bias,
        norm_gain,
        read_gain,
        out_weight,
    )


def solution(mesh):
    return jax.shard_map(
        functools.partial(body, mesh.shape["feat"], mesh.shape["head"]),
        mesh=mesh,
        in_specs=(
            P("groups"),
            P("head", "feat"),
            P(None, "groups", "head", "feat", None),
            P(None, "feat", "head"),
            P(None, "feat", "head"),
            P(None, "feat", "head"),
            P(None, "feat", "head"),
            P(None, "head"),
            P(None, "feat"),
            P(),
            P(None, "head", "feat"),
        ),
        out_specs=P("groups", "feat"),
        check_vma=False,
    )
```

time: 54.2 us -> 44.7 us (0.82)
  Pallas kernels: 52.4 us -> 43.8 us
  local copies, waits for them, and re-layouts: 1.4 us -> 0.62 us
    pallas_call x2, Pallas kernels: 52.4 us -> 43.8 us  [the longest x1 41 us: body(): pl.pallas_call(functools.partial(kernel, feat_count, head_count, parts),...]
    unnamed x1, local copies, waits for them, and re-layouts: 1.4 us -> 0.62 us
where the time goes in v1:
time: 44.7 us; the launch traced here: 44.4 us
  Pallas kernels  43.8 us (98%)
  local copies, waits for them, and re-layouts  0.62 us (1%)
    pallas_call x1, Pallas kernels, body(): pl.pallas_call(functools.partial(kernel, feat_count, head_count, parts),...  41 us
    pallas_call x1, Pallas kernels, body(): pl.pallas_call(lookup, out_shape=pltpu.VMEM((requests, width), BF16), in_...  2.77 us

profile of v1, /device:TPU:0, one launch (start us, length us, event | category | flops | bytes accessed | tf_op | source)
XLA Modules:
  0.0 44.4 jit_solution(17553614697402284930)
XLA Ops:
  0.0 2.8 %shard_map.109.picked_ref = bf16[16,1280]{1,0:T(8,128)(2,1)S(1)} custom-call(s32[16]{0:T(128)} %ids_ref.1, bf16[18992,1280]{1,0:T(8,128)(2,1)} %table_hbm.1), custom_call_target="tpu_custom_call" | custom-call | tf_op jit(solution)/shard_map/pallas_call | solution.py:401
  2.8 41.0 %shard_map.110 = bf16[16,1280]{1,0:T(8,128)(2,1)S(1)} custom-call(bf16[16,1280]{1,0:T(8,128)(2,1)S(1)} %shard_map.109.picked_ref, bf16[2,16,2,2064,128]{4,3,2,1,0:T(8,128)(2,1)} %retained_hbm.1, bf16[2,1280,1280]{2,1,0:T(8,128)(2,1)} %query_hbm.1, bf16[2,1280,256]{2,1,0:T(8,128)(2,1)} %key_hbm.1, bf16[2,1280,256]{2,1,0:T(8,128)(2,1)} %value_hbm.1, ...), custom_call_target="tpu_custom_call" | custom-call | tf_op jit(solution)/shard_map/pallas_call | solution.py:413
  43.8 0.6 %copy.13 = bf16[16,1280]{1,0:T(8,128)(2,1)} copy(bf16[16,1280]{1,0:T(8,128)(2,1)S(1)} %shard_map.110) | data formatting | bytes 81920

commit v2 on v1

--- a/solution.py
+++ b/solution.py
@@ -80,8 +80,8 @@
     pair_buf,
     read_buf,
     branch_buf,
-    left_sel,
-    right_sel,
+    left_at,
+    right_at,
     pair_scale,
     phi,
     history,
@@ -89,6 +89,7 @@
     state_sem,
     send_sem,
     recv_sem,
+    reach_sem,
 ):
     layers, requests, heads, block, head_size = state.shape
     width = query_w.shape[1]
@@ -101,12 +102,25 @@
     me_feat = lax.axis_index("feat")
     me_head = lax.axis_index("head")
 
+    last = feat_count - 1
     barrier = pltpu.get_barrier_semaphore()
-    for axis, count, me in (("feat", feat_count, me_feat), ("head", head_count, me_head)):
-        for d in range(1, count):
-            pl.semaphore_signal(
-                barrier, inc=1, device_id={axis: lax.rem(me + d, count)}, device_id_type=MESH
-            )
+    for d in range(1, head_count):
+        pl.semaphore_signal(
+            barrier, inc=1, device_id={"head": lax.rem(me_head + d, head_count)}, device_id_type=MESH
+        )
+
+    def tell(semaphore, condition, other):
+        @pl.when(condition)
+        def _():
+            pl.semaphore_signal(semaphore, inc=1, device_id={"feat": other}, device_id_type=MESH)
+
+    def hear(semaphore, condition):
+        @pl.when(condition)
+        def _():
+            pl.semaphore_wait(semaphore, 1)
+
+    tell(barrier, me_feat > 0, me_feat - 1)
+    tell(barrier, me_feat < last, me_feat + 1)
 
     load = {}
 
@@ -130,56 +144,68 @@
     start_load(6, bias_hbm, bias_ref, 0)
     start_load(7, read_hbm, read_ref, 0)
     load_inputs(0)
-    pl.semaphore_wait(barrier, feat_count + head_count - 2)
-
+    neighbours = jnp.minimum(me_feat, 1) + jnp.minimum(last - me_feat, 1)
+    pl.semaphore_wait(barrier, head_count - 1 + neighbours)
+
+    used = [0]
     sent = []
 
-    def exchange(axis, count, me, source, target):
-        copies = []
+    def exchange(axis, count, me, source, slots):
+        number = used[0]
+        used[0] += 1
         for d in range(1, count):
-            copy = pltpu.make_async_remote_copy(
+            pltpu.make_async_remote_copy(
                 src_ref=source,
-                dst_ref=target,
-                send_sem=send_sem.at[len(sent)],
-                recv_sem=recv_sem.at[len(sent)],
+                dst_ref=slots.at[me],
+                send_sem=send_sem.at[number],
+                recv_sem=recv_sem.at[number],
                 device_id={axis: partner_of(me, count, d)},
                 device_id_type=MESH,
-            )
-            copy.start()
-            copies.append(copy)
-            sent.append(copy)
-        return copies
-
-    def arrive(copies):
-        for copy in copies:
-            copy.wait_recv()
+            ).start()
+        others = slots.at[pl.ds(0, count - 1)]
+        sent.append(pltpu.make_async_copy(others, others, send_sem.at[number]))
+        return pltpu.make_async_copy(others, others, recv_sem.at[number])
+
+    def drain():
+        while sent:
+            sent.pop(0).wait()
 
     pick_copies = []
     for p in range(parts):
         rows = slice(p * n, (p + 1) * n)
         pick_copies.append(
             exchange(
-                "head", head_count, me_head, picked_ref.at[rows], pick_buf.at[p, me_head]
+                "head", head_count, me_head, picked_ref.at[rows], pick_buf.at[p]
             )
         )
+    tell(reach_sem.at[0], (me_feat == 1) & (me_feat < last), me_feat + 1)
+    tell(reach_sem.at[1], (me_feat == last - 1) & (me_feat > 0), me_feat - 1)
     load_state(0)
     for layer in range(1, layers):
         load_inputs(layer)
         load_state(layer)
 
-    feature = lax.broadcasted_iota(jnp.int32, (head_size, block), 1) + me_feat * block
-    position = lax.broadcasted_iota(jnp.int32, (head_size, block), 0)
-    begin = position * head_size - (position * (position - 1)) // 2
-    inside = (feature >= begin) & (feature < begin + head_size - position)
-    left_sel[...] = jnp.where(inside, 1.0, 0.0).astype(BF16)
-    partner = jnp.sum(jnp.where(inside, feature - begin + position, 0), axis=0, keepdims=True)
-    right_sel[...] = jnp.where(position == partner, 1.0, 0.0).astype(BF16)
-    first = jnp.sum(jnp.where(inside, position, 0), axis=0, keepdims=True)
-    pair_scale[...] = jnp.where(first == partner, 1.0, math.sqrt(2.0)).astype(F32)
+    position = lax.broadcasted_iota(jnp.int32, (head_size, LANES), 0)
+    begin = position * head_size - (position * (position - 1)) // 2 - me_feat * block
+    offset = lax.broadcasted_iota(jnp.int32, (n, LANES), 1)
+    for c in range(left_at.shape[0]):
+        reached = jnp.where(begin - lax.broadcasted_iota(jnp.int32, begin.shape, 1) <= c * LANES, 1, 0)
+        first = jnp.sum(reached, axis=0, keepdims=True) - 1
+        first = jnp.broadcast_to(first, (n, LANES))
+        start = first * head_size - (first * (first - 1)) // 2 - me_feat * block
+        second = jnp.minimum(offset + c * LANES - start + first, head_size - 1)
+        left_at[c] = first
+        right_at[c] = second
+        pair_scale[c] = jnp.where(first == second, 1.0, math.sqrt(2.0)).astype(F32)
     phi[...] = jnp.zeros(phi.shape, F32)
 
     for slot in (5, 6, 7):
         load[0, slot].wait()
+
+    hear(reach_sem.at[0], me_feat >= 2)
+    tell(reach_sem.at[0], (me_feat >= 2) & (me_feat < last), me_feat + 1)
+    hear(reach_sem.at[1], me_feat <= last - 2)
+    tell(reach_sem.at[1], (me_feat <= last - 2) & (me_feat > 0), me_feat - 1)
 
     fields = heads + 1
     lane = lax.broadcasted_iota(jnp.int32, (n, LANES), 1)
@@ -191,16 +217,18 @@
         pick_buf[p, me_head] = picked_ref[p * n : (p + 1) * n, :]
 
     for layer in range(layers):
-        lead_copies, query_copies, pair_copies = [], [], []
+        lead_copies, query_copies, gained_all = [], [], []
         for p in range(parts):
+            if p == 0:
+                drain()
             if layer == 0:
-                arrive(pick_copies[p])
+                pick_copies[p].wait()
                 total = pick_buf[p, 0].astype(F32)
                 for i in range(1, head_count):
                     total = total + pick_buf[p, i].astype(F32)
                 stream[p] = total
             else:
-                stream[p] = finish(p, layer - 1, stream, branch_copies, branch_buf, head_count, arrive)
+                stream[p] = finish(p, layer - 1, stream, branch_copies, branch_buf, head_count)
             gained = (stream[p] * gain_ref[layer : layer + 1, :]).astype(BF16)
             if p == 0:
                 load[layer, 0].wait()
@@ -223,28 +251,29 @@
             lead_buf[layer, p, me_feat, :, span:] = jnp.where(
                 lane < fields, high, jnp.where(lane < 2 * fields, middle, rest - middle)
             ).astype(BF16)
-            own = lead_buf.at[layer, p, me_feat]
-            lead_copies.append(exchange("feat", feat_count, me_feat, own, own))
+            slots = lead_buf.at[layer, p]
+            lead_copies.append(exchange("feat", feat_count, me_feat, slots.at[me_feat], slots))
             copies = []
             for h in range(1, heads):
                 query_buf[layer, p, h - 1, me_feat] = jnp.dot(
                     gained, query_w[layer, :, h * span : (h + 1) * span], preferred_element_type=F32
                 ).astype(BF16)
-                own = query_buf.at[layer, p, h - 1, me_feat]
-                copies.append(exchange("feat", feat_count, me_feat, own, own))
+                slots = query_buf.at[layer, p, h - 1]
+                copies.append(exchange("feat", feat_count, me_feat, slots.at[me_feat], slots))
             query_copies.append(copies)
-            for slot, weight in ((2, key_w), (3, value_w)):
-                if p == 0:
-                    load[layer, slot].wait()
-                pair_buf[layer, p, me_feat, :, (slot - 2) * kv_columns : (slot - 1) * kv_columns] = (
-                    jnp.dot(gained, weight[layer], preferred_element_type=F32).astype(BF16)
-                )
-            own = pair_buf.at[layer, p, me_feat]
-            pair_copies.append(exchange("feat", feat_count, me_feat, own, own))
+            gained_all.append(gained)
+        gained = jnp.concatenate(gained_all, axis=0)
+        for slot, weight in ((2, key_w), (3, value_w)):
+            load[layer, slot].wait()
+            pair_buf[layer, me_feat, :, (slot - 2) * kv_columns : (slot - 1) * kv_columns] = jnp.dot(
+                gained, weight[layer], preferred_element_type=F32
+            ).astype(BF16)
+        slots = pair_buf.at[layer]
+        pair_copies = exchange("feat", feat_count, me_feat, slots.at[me_feat], slots)
 
         query, decay, inverse, read_copies = [], [], [], []
         for p in range(parts):
-            arrive(lead_copies[p])
+            lead_copies[p].wait()
             totals = lead_buf[layer, p, 0, :, span:].astype(F32)
             for i in range(1, feat_count):
                 totals = totals + lead_buf[layer, p, i, :, span:].astype(F32)
@@ -258,57 +287,60 @@
             decay.append(1.0 / (1.0 + jnp.exp(gate)))
             query.append([])
             read_copies.append([])
-            for h in range(heads):
+
+            def features(h):
                 if h == 0:
                     summed = lead_buf[layer, p, 0, :, :span].astype(F32)
                     for i in range(1, feat_count):
                         summed = summed + lead_buf[layer, p, i, :, :span].astype(F32)
                 else:
-                    arrive(query_copies[p][h - 1])
+                    query_copies[p][h - 1].wait()
                     summed = query_buf[layer, p, h - 1, 0].astype(F32)
                     for i in range(1, feat_count):
                         summed = summed + query_buf[layer, p, h - 1, i].astype(F32)
-                summed = summed * inverse[p]
+                summed = (summed * inverse[p]).astype(BF16).astype(F32)
                 rows = [summed[:, i * head_size : (i + 1) * head_size] for i in range(group)]
-                stacked = jnp.concatenate(rows, axis=0).astype(BF16)
-                query[p].append([row.astype(BF16).astype(F32) for row in rows])
-                for start in range(0, block, 256):
-                    stop = min(start + 256, block)
-                    left = jnp.dot(stacked, left_sel[:, start:stop], preferred_element_type=F32)
-                    right = jnp.dot(stacked, right_sel[:, start:stop], preferred_element_type=F32)
-                    value = left * right * pair_scale[:, start:stop]
-                    for lo in range(start, stop, LANES):
-                        hi = min(lo + LANES, stop)
-                        phi[lo // LANES, : group * n, : hi - lo] = value[:, lo - start : hi - start]
-
-                def read(step, carry, h=h, p=p):
+                query[p].append(rows)
+                for c in range(left_at.shape[0]):
+                    first, second, scale = left_at[c], right_at[c], pair_scale[c]
+                    for i, row in enumerate(rows):
+                        left = jnp.take_along_axis(row, first, axis=1)
+                        right = jnp.take_along_axis(row, second, axis=1)
+                        phi[h % 2, c, i * n : (i + 1) * n, :] = left * right * scale
+
+            features(0)
+            for h in range(heads):
+                for step in range(n // unroll):
                     if h == 0:
                         for extra in range(unroll):
                             r = p * n + step * unroll + extra
                             pltpu.make_async_copy(
                                 retained_hbm.at[layer, r], state.at[layer, r], state_sem.at[layer, r]
                             ).wait()
+                    if h + 1 < heads and step == n // unroll - 1:
+                        features(h + 1)
                     for extra in range(unroll):
                         i = step * unroll + extra
                         at = pl.ds(i, 8, stride=n)
                         lhs = jnp.concatenate(
-                            [phi[c, at, :] for c in range(phi.shape[0])], axis=1
+                            [phi[h % 2, c, at, :] for c in range(phi.shape[1])], axis=1
                         )[:, :block]
                         history[at, :] = jnp.dot(
                             lhs.astype(BF16), state[layer, p * n + i, h], preferred_element_type=F32
                         )
-                    return carry
-
-                lax.fori_loop(0, n // unroll, read, 0)
                 read_buf[layer, p, h, me_feat] = history[: group * n, :].astype(BF16)
-                own = read_buf.at[layer, p, h, me_feat]
-                read_copies[p].append(exchange("feat", feat_count, me_feat, own, own))
+                slots = read_buf.at[layer, p, h]
+                read_copies[p].append(
+                    exchange("feat", feat_count, me_feat, slots.at[me_feat], slots)
+                )
 
         for p in range(parts):
-            arrive(pair_copies[p])
-            summed = pair_buf[layer, p, 0].astype(F32)
+            if p == 0:
+                pair_copies.wait()
+            rows = slice(p * n, (p + 1) * n)
+            summed = pair_buf[layer, 0, rows].astype(F32)
             for i in range(1, feat_count):
-                summed = summed + pair_buf[layer, p, i].astype(F32)
+                summed = summed + pair_buf[layer, i, rows].astype(F32)
             summed = (summed * inverse[p]).astype(BF16).astype(F32)
             if p == 0:
                 load[layer, 4].wait()
@@ -321,7 +353,7 @@
                 for i in range(group):
                     along = jnp.sum(query[p][h][i] * key, axis=1, keepdims=True)
                     cross.append(along * along / head_size)
-                arrive(read_copies[p][h])
+                read_copies[p][h].wait()
                 reads = read_buf[layer, p, h, 0].astype(F32)
                 for i in range(1, feat_count):
                     reads = reads + read_buf[layer, p, h, i].astype(F32)
@@ -345,21 +377,22 @@
                     pieces.append(part)
                     if h == heads - 1:
                         branch_buf[layer, p, c, me_head] = part.astype(BF16)
-                        own = branch_buf.at[layer, p, c, me_head]
-                        branch_copies[p].append(exchange("head", head_count, me_head, own, own))
+                        slots = branch_buf.at[layer, p, c]
+                        branch_copies[p].append(
+                            exchange("head", head_count, me_head, slots.at[me_head], slots)
+                        )
                 partial = pieces
 
     for p in range(parts):
-        done = finish(p, layers - 1, stream, branch_copies, branch_buf, head_count, arrive)
+        done = finish(p, layers - 1, stream, branch_copies, branch_buf, head_count)
         result_ref[p * n : (p + 1) * n, :] = done.astype(BF16)
-    for copy in sent:
-        copy.wait_send()
-
-
-def finish(p, layer, stream, branch_copies, branch_buf, head_count, arrive):
+    drain()
+
+
+def finish(p, layer, stream, branch_copies, branch_buf, head_count):
     branch = []
     for c in range(len(branch_copies[p])):
-        arrive(branch_copies[p][c])
+        branch_copies[p][c].wait()
         total = branch_buf[layer, p, c, 0].astype(F32)
         for i in range(1, head_count):
             total = total + branch_buf[layer, p, c, i].astype(F32)
@@ -391,11 +424,8 @@
     span = group * head_size
     parts = 2 if requests % 16 == 0 else 1
     n = requests // parts
-    chunks = 1
-    copies = parts * (
-        (head_count - 1)
-        + layers * ((1 + 2 * heads) * (feat_count - 1) + chunks * (head_count - 1))
-    )
+    chunks = 2 if width % 256 == 0 else 1
+    copies = parts + layers * (1 + parts * (2 * heads + chunks))
     gate_rows = jnp.swapaxes(gate_weight, 1, 2)
     window = 16
     picked = pl.pallas_call(
@@ -428,18 +458,19 @@
             pltpu.VMEM((parts, head_count, n, width), BF16),
             pltpu.VMEM((layers, parts, feat_count, n, span + LANES), BF16),
             pltpu.VMEM((layers, parts, max(heads - 1, 1), feat_count, n, span), BF16),
-            pltpu.VMEM((layers, parts, feat_count, n, 2 * kv_columns), BF16),
+            pltpu.VMEM((layers, feat_count, requests, 2 * kv_columns), BF16),
             pltpu.VMEM((layers, parts, heads, feat_count, n * group, head_size), BF16),
             pltpu.VMEM((layers, parts, chunks, head_count, n, width // chunks), BF16),
-            pltpu.VMEM((head_size, block), BF16),
-            pltpu.VMEM((head_size, block), BF16),
-            pltpu.VMEM((1, block), F32),
-            pltpu.VMEM((pl.cdiv(block, LANES), 8 * n, LANES), F32),
+            pltpu.VMEM((pl.cdiv(block, LANES), n, LANES), jnp.int32),
+            pltpu.VMEM((pl.cdiv(block, LANES), n, LANES), jnp.int32),
+            pltpu.VMEM((pl.cdiv(block, LANES), n, LANES), F32),
+            pltpu.VMEM((2, pl.cdiv(block, LANES), 8 * n, LANES), F32),
             pltpu.VMEM((8 * n, head_size), F32),
             pltpu.SemaphoreType.DMA((layers, 8)),
             pltpu.SemaphoreType.DMA((layers, requests)),
             pltpu.SemaphoreType.DMA((copies,)),
             pltpu.SemaphoreType.DMA((copies,)),
+            pltpu.SemaphoreType.REGULAR((2,)),
         ],
         compiler_params=pltpu.CompilerParams(
             collective_id=0, has_side_effects=True, vmem_limit_bytes=66_000_000

time: 44.7 us -> 41.7 us (0.933)
  Pallas kernels: 43.8 us -> 40.8 us
    pallas_call x1, Pallas kernels: 41 us -> 38.2 us  [body(): pl.pallas_call(functools.partial(kernel, feat_count, head_count, parts),...]
where the time goes in v2:
time: 41.7 us; the launch traced here: 41.5 us
  Pallas kernels  40.8 us (98%)
  local copies, waits for them, and re-layouts  0.62 us (1%)
    pallas_call x1, Pallas kernels, body(): pl.pallas_call(functools.partial(kernel, feat_count, head_count, parts),...  38.2 us
    pallas_call x1, Pallas kernels, body(): pl.pallas_call(lookup, out_shape=pltpu.VMEM((requests, width), BF16), in_...  2.63 us

profile of v2, /device:TPU:0, one launch (start us, length us, event | category | flops | bytes accessed | tf_op | source)
XLA Modules:
  0.0 41.5 jit_solution(1921991998983927179)
XLA Ops:
  0.0 2.6 %shard_map.109.picked_ref = bf16[16,1280]{1,0:T(8,128)(2,1)S(1)} custom-call(s32[16]{0:T(128)} %ids_ref.1, bf16[18992,1280]{1,0:T(8,128)(2,1)} %table_hbm.1), custom_call_target="tpu_custom_call" | custom-call | tf_op jit(solution)/shard_map/pallas_call | solution.py:431
  2.6 38.2 %shard_map.110 = bf16[16,1280]{1,0:T(8,128)(2,1)S(1)} custom-call(bf16[16,1280]{1,0:T(8,128)(2,1)S(1)} %shard_map.109.picked_ref, bf16[2,16,2,2064,128]{4,3,2,1,0:T(8,128)(2,1)} %retained_hbm.1, bf16[2,1280,1280]{2,1,0:T(8,128)(2,1)} %query_hbm.1, bf16[2,1280,256]{2,1,0:T(8,128)(2,1)} %key_hbm.1, bf16[2,1280,256]{2,1,0:T(8,128)(2,1)} %value_hbm.1, ...), custom_call_target="tpu_custom_call" | custom-call | tf_op jit(solution)/shard_map/pallas_call | solution.py:443
  40.8 0.6 %copy.13 = bf16[16,1280]{1,0:T(8,128)(2,1)} copy(bf16[16,1280]{1,0:T(8,128)(2,1)S(1)} %shard_map.110) | data formatting | bytes 81920

commit v3 on v2

--- a/solution.py
+++ b/solution.py
@@ -14,36 +14,6 @@
 LANES = 128
 
 
-def lookup(ids_ref, table_hbm, picked_ref, rows_buf, row_sem):
-    requests, width = picked_ref.shape
-    table_rows = table_hbm.shape[0]
-    base = lax.axis_index("head") * table_rows
-    window = rows_buf.shape[0] // requests
-    out_row = lax.broadcasted_iota(jnp.int32, (requests, requests * window), 0)
-    column = lax.broadcasted_iota(jnp.int32, (requests, requests * window), 1)
-    select = jnp.zeros((requests, requests * window), F32)
-    copies = []
-    for i in range(requests):
-        local = ids_ref[i] - base
-        row = jnp.clip(local, 0, table_rows - 1)
-        first = pl.multiple_of(jnp.minimum((row // 8) * 8, table_rows - window), 8)
-        copy = pltpu.make_async_copy(
-            table_hbm.at[pl.ds(first, window)],
-            rows_buf.at[pl.ds(i * window, window)],
-            row_sem.at[i],
-        )
-        copy.start()
-        copies.append(copy)
-        value = jnp.where(local == row, 1.0, 0.0)
-        hit = (out_row == i) & (column == i * window + row - first)
-        select = jnp.where(hit, value, select)
-    for copy in copies:
-        copy.wait()
-    picked_ref[...] = jnp.dot(
-        select.astype(BF16), rows_buf[...], preferred_element_type=F32
-    ).astype(BF16)
-
-
 def partner_of(me, count, turn):
     if count == 4:
         return (3 - me, lax.rem(me + 2, 4), me + 1 - 2 * lax.rem(me, 2))[turn - 1]
@@ -54,6 +24,8 @@
     feat_count,
     head_count,
     parts,
+    table_rows,
+    ids_hbm,
     picked_ref,
     retained_hbm,
     query_hbm,
@@ -65,6 +37,7 @@
     read_hbm,
     out_hbm,
     result_ref,
+    ids_ref,
     state,
     query_w,
     key_w,
@@ -94,7 +67,6 @@
     layers, requests, heads, block, head_size = state.shape
     width = query_w.shape[1]
     query_columns = query_w.shape[2]
-    kv_columns = key_w.shape[2]
     chunks, chunk = branch_buf.shape[2], branch_buf.shape[5]
     group = query_columns // (heads * head_size)
     span = group * head_size
@@ -140,6 +112,7 @@
             ).start()
         start_load(4, out_hbm.at[layer], out_w.at[layer], layer)
 
+    start_load(8, ids_hbm, ids_ref, 0)
     start_load(5, gain_hbm, gain_ref, 0)
     start_load(6, bias_hbm, bias_ref, 0)
     start_load(7, read_hbm, read_ref, 0)
@@ -163,12 +136,37 @@
                 device_id_type=MESH,
             ).start()
         others = slots.at[pl.ds(0, count - 1)]
-        sent.append(pltpu.make_async_copy(others, others, send_sem.at[number]))
+        sent.append(pltpu.make_async_copy(others, others, send_sem.at[number]).wait)
         return pltpu.make_async_copy(others, others, recv_sem.at[number])
 
-    def drain():
-        while sent:
-            sent.pop(0).wait()
+    def collect(axis, count, me, owner, slots):
+        number = used[0]
+        used[0] += 1
+        mine = slots.at[me]
+        others = slots.at[pl.ds(0, count - 1)]
+
+        @pl.when(me != owner)
+        def _():
+            pltpu.make_async_remote_copy(
+                src_ref=mine,
+                dst_ref=mine,
+                send_sem=send_sem.at[number],
+                recv_sem=recv_sem.at[number],
+                device_id={axis: owner},
+                device_id_type=MESH,
+            ).start()
+
+        def finished():
+            @pl.when(me != owner)
+            def _():
+                pltpu.make_async_copy(mine, mine, send_sem.at[number]).wait()
+
+        sent.append(finished)
+        return pltpu.make_async_copy(others, others, recv_sem.at[number])
+
+    def drain(number):
+        for _ in range(number):
+            sent.pop(0)()
 
     pick_copies = []
     for p in range(parts):
@@ -199,7 +197,7 @@
         pair_scale[c] = jnp.where(first == second, 1.0, math.sqrt(2.0)).astype(F32)
     phi[...] = jnp.zeros(phi.shape, F32)
 
-    for slot in (5, 6, 7):
+    for slot in (5, 6, 7, 8):
         load[0, slot].wait()
 
     hear(reach_sem.at[0], me_feat >= 2)
@@ -208,6 +206,7 @@
     tell(reach_sem.at[1], (me_feat <= last - 2) & (me_feat > 0), me_feat - 1)
 
     fields = heads + 1
+    owners = [(max(feat_count // 2, 1) - 1 + h) % feat_count for h in range(heads)]
     lane = lax.broadcasted_iota(jnp.int32, (n, LANES), 1)
     unroll = 4 if n % 4 == 0 else 1
     stream = [None] * parts
@@ -217,15 +216,19 @@
         pick_buf[p, me_head] = picked_ref[p * n : (p + 1) * n, :]
 
     for layer in range(layers):
-        lead_copies, query_copies, gained_all = [], [], []
+        lead_copies, query_copies, pair_copies = [], [], []
+        earlier = len(sent)
         for p in range(parts):
-            if p == 0:
-                drain()
             if layer == 0:
                 pick_copies[p].wait()
-                total = pick_buf[p, 0].astype(F32)
-                for i in range(1, head_count):
-                    total = total + pick_buf[p, i].astype(F32)
+                token = jnp.zeros((n, 1), jnp.int32)
+                line = lax.broadcasted_iota(jnp.int32, (n, 1), 0)
+                for i in range(n):
+                    token = jnp.where(line == i, ids_ref[p * n + i], token)
+                total = jnp.zeros((n, width), F32)
+                for i in range(head_count):
+                    mine = (token >= i * table_rows) & (token < (i + 1) * table_rows)
+                    total = jnp.where(mine, pick_buf[p, i].astype(F32), total)
                 stream[p] = total
             else:
                 stream[p] = finish(p, layer - 1, stream, branch_copies, branch_buf, head_count)
@@ -261,16 +264,22 @@
                 slots = query_buf.at[layer, p, h - 1]
                 copies.append(exchange("feat", feat_count, me_feat, slots.at[me_feat], slots))
             query_copies.append(copies)
-            gained_all.append(gained)
-        gained = jnp.concatenate(gained_all, axis=0)
-        for slot, weight in ((2, key_w), (3, value_w)):
-            load[layer, slot].wait()
-            pair_buf[layer, me_feat, :, (slot - 2) * kv_columns : (slot - 1) * kv_columns] = jnp.dot(
-                gained, weight[layer], preferred_element_type=F32
-            ).astype(BF16)
-        slots = pair_buf.at[layer]
-        pair_copies = exchange("feat", feat_count, me_feat, slots.at[me_feat], slots)
-
+            for slot, weight in ((2, key_w), (3, value_w)):
+                if p == 0:
+                    load[layer, slot].wait()
+                product = jnp.dot(gained, weight[layer], preferred_element_type=F32).astype(BF16)
+                for h in range(heads):
+                    pair_buf[layer, p, h, me_feat, :, (slot - 2) * head_size : (slot - 1) * head_size] = (
+                        product[:, h * head_size : (h + 1) * head_size]
+                    )
+            pair_copies.append(
+                [
+                    collect("feat", feat_count, me_feat, owners[h], pair_buf.at[layer, p, h])
+                    for h in range(heads)
+                ]
+            )
+
+        drain(earlier)
         query, decay, inverse, read_copies = [], [], [], []
         for p in range(parts):
             lead_copies[p].wait()
@@ -328,40 +337,46 @@
                         history[at, :] = jnp.dot(
                             lhs.astype(BF16), state[layer, p * n + i, h], preferred_element_type=F32
                         )
-                read_buf[layer, p, h, me_feat] = history[: group * n, :].astype(BF16)
+                kept = jnp.concatenate([decay[p][:, h : h + 1]] * group, axis=0)
+                kept = kept * history[: group * n, :]
+
+                @pl.when(me_feat != owners[h])
+                def _():
+                    read_buf[layer, p, h, me_feat] = kept.astype(BF16)
+
+                @pl.when(me_feat == owners[h])
+                def _():
+                    pair_copies[p][h].wait()
+                    summed = pair_buf[layer, p, h, 0].astype(F32)
+                    for i in range(1, feat_count):
+                        summed = summed + pair_buf[layer, p, h, i].astype(F32)
+                    summed = (summed * inverse[p]).astype(BF16).astype(F32)
+                    key, value = summed[:, :head_size], summed[:, head_size:]
+                    fresh = []
+                    for row in query[p][h]:
+                        along = jnp.sum(row * key, axis=1, keepdims=True)
+                        fresh.append(along * along / head_size * value)
+                    fresh = jnp.concatenate(fresh, axis=0)
+                    read_buf[layer, p, h, me_feat] = (kept + fresh).astype(BF16)
+
                 slots = read_buf.at[layer, p, h]
                 read_copies[p].append(
                     exchange("feat", feat_count, me_feat, slots.at[me_feat], slots)
                 )
 
         for p in range(parts):
-            if p == 0:
-                pair_copies.wait()
-            rows = slice(p * n, (p + 1) * n)
-            summed = pair_buf[layer, 0, rows].astype(F32)
-            for i in range(1, feat_count):
-                summed = summed + pair_buf[layer, i, rows].astype(F32)
-            summed = (summed * inverse[p]).astype(BF16).astype(F32)
             if p == 0:
                 load[layer, 4].wait()
             branch_copies[p] = []
             partial = None
             for h in range(heads):
-                key = summed[:, h * head_size : (h + 1) * head_size]
-                value = summed[:, kv_columns + h * head_size : kv_columns + (h + 1) * head_size]
-                cross = []
-                for i in range(group):
-                    along = jnp.sum(query[p][h][i] * key, axis=1, keepdims=True)
-                    cross.append(along * along / head_size)
                 read_copies[p][h].wait()
                 reads = read_buf[layer, p, h, 0].astype(F32)
                 for i in range(1, feat_count):
                     reads = reads + read_buf[layer, p, h, i].astype(F32)
                 mixed = []
                 for i in range(group):
-                    readout = (
-                        decay[p][:, h : h + 1] * reads[i * n : (i + 1) * n] + cross[i] * value
-                    )
+                    readout = reads[i * n : (i + 1) * n]
                     scale = lax.rsqrt(jnp.mean(readout * readout, axis=1, keepdims=True) + 1e-06)
                     mixed.append((readout * scale * read_ref[layer : layer + 1, :]).astype(BF16))
                 mixed = jnp.concatenate(mixed, axis=1)
@@ -386,7 +401,7 @@
     for p in range(parts):
         done = finish(p, layers - 1, stream, branch_copies, branch_buf, head_count)
         result_ref[p * n : (p + 1) * n, :] = done.astype(BF16)
-    drain()
+    drain(len(sent))
 
 
 def finish(p, layer, stream, branch_copies, branch_buf, head_count):
@@ -419,33 +434,32 @@
     layers, requests, heads, block, head_size = retained.shape
     width = query_weight.shape[1]
     query_columns = query_weight.shape[2]
-    kv_columns = key_weight.shape[2]
     group = query_columns // (heads * head_size)
     span = group * head_size
     parts = 2 if requests % 16 == 0 else 1
     n = requests // parts
     chunks = 2 if width % 256 == 0 else 1
-    copies = parts + layers * (1 + parts * (2 * heads + chunks))
+    copies = parts + layers * parts * (3 * heads + chunks)
     gate_rows = jnp.swapaxes(gate_weight, 1, 2)
-    window = 16
-    picked = pl.pallas_call(
-        lookup,
-        out_shape=pltpu.VMEM((requests, width), BF16),
-        in_specs=[pl.BlockSpec(memory_space=pltpu.SMEM), pl.BlockSpec(memory_space=pl.ANY)],
-        out_specs=pl.BlockSpec(memory_space=pltpu.VMEM),
-        scratch_shapes=[
-            pltpu.VMEM((requests * window, width), BF16),
-            pltpu.SemaphoreType.DMA((requests,)),
-        ],
-    )(token_ids, embedding)
+    local_row = token_ids - lax.axis_index("head") * embedding.shape[0]
+    picked = lax.gather(
+        embedding,
+        local_row[:, None],
+        lax.GatherDimensionNumbers(
+            offset_dims=(1,), collapsed_slice_dims=(0,), start_index_map=(0,)
+        ),
+        slice_sizes=(1, width),
+        mode=lax.GatherScatterMode.CLIP,
+    )
     anywhere = pl.BlockSpec(memory_space=pl.ANY)
     local = pl.BlockSpec(memory_space=pltpu.VMEM)
     return pl.pallas_call(
-        functools.partial(kernel, feat_count, head_count, parts),
+        functools.partial(kernel, feat_count, head_count, parts, embedding.shape[0]),
         out_shape=pltpu.VMEM((requests, width), BF16),
-        in_specs=[local] + [anywhere] * 9,
+        in_specs=[anywhere, local] + [anywhere] * 9,
         out_specs=local,
         scratch_shapes=[
+            pltpu.SMEM(token_ids.shape, jnp.int32),
             pltpu.VMEM(retained.shape, BF16),
             pltpu.VMEM(query_weight.shape, BF16),
             pltpu.VMEM(key_weight.shape, BF16),
@@ -458,7 +472,7 @@
             pltpu.VMEM((parts, head_count, n, width), BF16),
             pltpu.VMEM((layers, parts, feat_count, n, span + LANES), BF16),
             pltpu.VMEM((layers, parts, max(heads - 1, 1), feat_count, n, span), BF16),
-            pltpu.VMEM((layers, feat_count, requests, 2 * kv_columns), BF16),
+            pltpu.VMEM((layers, parts, heads, feat_count, n, 2 * head_size), BF16),
             pltpu.VMEM((layers, parts, heads, feat_count, n * group, head_size), BF16),
             pltpu.VMEM((layers, parts, chunks, head_count, n, width // chunks), BF16),
             pltpu.VMEM((pl.cdiv(block, LANES), n, LANES), jnp.int32),
@@ -466,7 +480,7 @@
             pltpu.VMEM((pl.cdiv(block, LANES), n, LANES), F32),
             pltpu.VMEM((2, pl.cdiv(block, LANES), 8 * n, LANES), F32),
             pltpu.VMEM((8 * n, head_size), F32),
-            pltpu.SemaphoreType.DMA((layers, 8)),
+            pltpu.SemaphoreType.DMA((layers, 9)),
             pltpu.SemaphoreType.DMA((layers, requests)),
             pltpu.SemaphoreType.DMA((copies,)),
             pltpu.SemaphoreType.DMA((copies,)),
@@ -476,6 +490,7 @@
             collective_id=0, has_side_effects=True, vmem_limit_bytes=66_000_000
         ),
     )(
+        token_ids,
         pltpu.with_memory_space_constraint(picked, pltpu.VMEM),
         retained,
         query_weight,

time: 41.7 us -> 40.3 us (0.966)
  Pallas kernels: 40.8 us -> 37.2 us
  local copies, waits for them, and re-layouts: 0.62 us -> 2.28 us
  other arithmetic: 0 us -> 0.67 us
    pallas_call x2 -> x1, Pallas kernels: 40.8 us -> 37.2 us  [body(): pl.pallas_call(functools.partial(kernel, feat_count, head_count, parts, e...]
    gather x0 -> x1, local copies, waits for them, and re-layouts: none -> 1.66 us  [body(): lax.gather(embedding, local_row[:, None], lax.GatherDimensionNumbers(offs...]
    sub x0 -> x1, other arithmetic: none -> 0.66 us  [body(): local_row = token_ids - lax.axis_index('head') * embedding.shape[0]]
where the time goes in v3:
time: 40.3 us; the launch traced here: 40.2 us
  Pallas kernels  37.2 us (92%)
  local copies, waits for them, and re-layouts  2.28 us (6%)
  other arithmetic  0.67 us (2%)
    pallas_call x1, Pallas kernels, body(): pl.pallas_call(functools.partial(kernel, feat_count, head_count, parts, e...  37.2 us
    gather x1, local copies, waits for them, and re-layouts, body(): lax.gather(embedding, local_row[:, None], lax.GatherDimensionNumbers(offs...  1.66 us

profile of v3, /device:TPU:0, one launch (start us, length us, event | category | flops | bytes accessed | tf_op | source)
XLA Modules:
  0.0 40.2 jit_solution(18195325048847243130)
XLA Ops:
  0.0 0.7 %broadcast_subtract_fusion = s32[16]{0:T(128)S(1)} fusion(s32[16]{0:T(128)} %ids_hbm.1, s32[]{:T(128)S(6)} %mul.3), kind=kLoop, calls=%fused_computation.2 | loop fusion | flops 16 | bytes 132 | tf_op jit(solution)/shard_map/sub | solution.py:444
  0.7 1.7 %gather_fusion = bf16[16,1280]{1,0:T(8,128)(2,1)S(1)} fusion(bf16[18992,1280]{1,0:T(8,128)(2,1)} %param.12, s32[1024]{0:T(1024)S(1)} %pad_clamp_fusion), kind=kCustom, calls=%fused_computation | custom fusion | bytes 81984 | tf_op jit(solution)/shard_map/gather | solution.py:445
  2.3 37.2 %shard_map.109 = bf16[16,1280]{1,0:T(8,128)(2,1)S(1)} custom-call(s32[16]{0:T(128)} %ids_hbm.1, bf16[16,1280]{1,0:T(8,128)(2,1)S(1)} %gather_fusion, bf16[2,16,2,2064,128]{4,3,2,1,0:T(8,128)(2,1)} %retained_hbm.1, bf16[2,1280,1280]{2,1,0:T(8,128)(2,1)} %query_hbm.1, bf16[2,1280,256]{2,1,0:T(8,128)(2,1)} %key_hbm.1, bf16[2,1280,256]{2,1,0:T(8,128)(2,1)} %value_hbm.1, ...), custom_call_target="tpu_custom_call" | custom-call | tf_op jit(solution)/shard_map/pallas_call | solution.py:456
  39.5 0.6 %copy.13 = bf16[16,1280]{1,0:T(8,128)(2,1)} copy(bf16[16,1280]{1,0:T(8,128)(2,1)S(1)} %shard_map.109) | data formatting | bytes 81920
  (1 shorter events, 0.0 us)
